TPU v7x, 128 devices: a whole 4x4x4 slice. The times are simulated.
128 devices in a mesh: segment: 2 (over z_hi), win: 16 (over y, z_lo, core), head: 4 (over x).
Axes of the slice: x: 4, y: 4, z: 4 (z_hi: 2, z_lo: 2; z = z_hi * 2 + z_lo), core: 2. Of those that a mesh axis runs over, the one named last changes fastest.
Arguments:
- inputs: bfloat16 [2, 30, 480, 1536], P(None, None, 'win', 'head'), may hold values from -16 to 16
- gains: float32 [2, 1536], P('segment'), may hold values from 0.1 to 1.9
- qkv_weight: bfloat16 [2, 1536, 3, 1536], P('segment', None, None, 'head'), may hold values from -3.5 to 3.5
- out_weight: bfloat16 [2, 1536, 1536], P('segment', 'head'), may hold values from -0.15625 to 0.15625
- labels: int32 [30, 480], P(None, 'win'), may hold values from 0 to 3, as said below
Outputs:
- sections: bfloat16 [2, 2, 30, 480, 1536], P('segment', None, None, 'win', 'head')
Inputs may be any that keep to these rules, and one draw needn't show every extreme that they name: In each window of 30 by 30 cells the label is 2 on the rows from a drawn row cut on plus 1 on the columns from a drawn column cut on; both cuts lie in 1 to 29, so every window holds all four labels.
All inputs are finite; a program needn't handle non-finite values.
Results may differ from a plain program's by a relative error of at most 0.013.
Values may be sent and summed in bfloat16 or wider, within the bound.
No kernel may reach another device: no remote copies, remote signals or barrier semaphores. Data moves between devices by JAX's collectives and lax.ppermute only.
A program may use at most 128 MiB of HBM per device.

v0:
```python
import jax
import jax.numpy as jnp
from jax import lax
from jax.sharding import PartitionSpec as P

HEAD_DIM = 128
WIN_SIDE = 30


def passed_along(array, axis, by):
    length = lax.axis_size(axis)
    return lax.ppermute(array, axis, [(i, (i + by) % length) for i in range(length)])


def shifted(value, axis, steps):
    count = lax.axis_size(axis)
    first, last = (max(0, -steps), min(count, count - steps))
    return lax.ppermute(value, axis, [(source, source + steps) for source in range(first, last)])


def rms_normed(slab, gain_row):
    values_f = slab.astype(jnp.float32)
    mean_square = jnp.mean(values_f * values_f, axis=-1, keepdims=True)
    return (values_f * lax.rsqrt(mean_square + 1e-05) * gain_row).astype(jnp.bfloat16)


def to_windows(grid):
    win_rows = grid.shape[0]
    win_count = grid.shape[1] // win_rows
    features = grid.shape[2]
    return (
        grid.reshape(win_rows, win_count, win_rows, features)
        .transpose(1, 0, 2, 3)
        .reshape(win_count, win_rows * win_rows, features)
    )


def from_windows(blocks, win_rows):
    win_count = blocks.shape[0]
    features = blocks.shape[2]
    return (
        blocks.reshape(win_count, win_rows, win_rows, features)
        .transpose(1, 0, 2, 3)
        .reshape(win_rows, win_count * win_rows, features)
    )


def window_layer(current, gain_row, qkv_local, allowed, project):
    gathered = lax.all_gather(current, "head", axis=2, tiled=True)
    normed = rms_normed(gathered, gain_row)
    win_normed = to_windows(normed)
    projected_qkv = jnp.einsum(
        "wtd,dcf->wtcf", win_normed, qkv_local, preferred_element_type=jnp.float32
    ).astype(jnp.bfloat16)
    win_count = projected_qkv.shape[0]
    tokens = projected_qkv.shape[1]
    local_feat = projected_qkv.shape[3]
    heads_local = local_feat // HEAD_DIM
    split_qkv = projected_qkv.reshape(win_count, tokens, 3, heads_local, HEAD_DIM)
    queries = split_qkv[:, :, 0]
    keys_all = split_qkv[:, :, 1]
    values_all = split_qkv[:, :, 2]
    scores = jnp.einsum(
        "wqhe,wkhe->whqk", queries, keys_all, preferred_element_type=jnp.float32
    ) * HEAD_DIM ** (-0.5)
    scores = jnp.where(allowed[:, None], scores, -1e30)
    top_score = jnp.max(scores, axis=-1, keepdims=True)
    expo = jnp.exp(scores - top_score)
    attn_prob = (expo / jnp.sum(expo, axis=-1, keepdims=True)).astype(jnp.bfloat16)
    attended = jnp.einsum(
        "whqk,wkhe->wqhe", attn_prob, values_all, preferred_element_type=jnp.float32
    ).astype(jnp.bfloat16)
    attended = attended.reshape(win_count, tokens, local_feat)
    grid_att = from_windows(attended, current.shape[0])
    projected = project(grid_att)
    return (current.astype(jnp.float32) + projected).astype(jnp.bfloat16)


def body(inputs, gains, qkv_weight, out_weight, labels):
    segment_id = lax.axis_index("segment")
    micro_count = inputs.shape[0]
    gain_row = gains[0]
    qkv_local = qkv_weight[0]
    out_local = out_weight[0]
    win_labels = to_windows(labels[:, :, None])[:, :, 0]
    allowed = (win_labels[:, :, None] == win_labels[:, None, :]) | (segment_id == 0)
    half_cols = WIN_SIDE // 2

    def project(grid_att):
        partial_sum = jnp.einsum(
            "rcf,fg->rcg", grid_att, out_local, preferred_element_type=jnp.float32
        )
        return lax.psum_scatter(
            partial_sum.astype(jnp.bfloat16), "head", scatter_dimension=2, tiled=True
        ).astype(jnp.float32)

    def advance(incoming, step_id):
        fresh = lax.dynamic_index_in_dim(
            inputs, jnp.minimum(step_id, micro_count - 1), 0, keepdims=False
        )
        current = jnp.where(segment_id == 0, fresh, incoming)
        leading = passed_along(current[:, :half_cols], "win", -1)
        rolled = jnp.concatenate([current[:, half_cols:], leading], axis=1)
        current = jnp.where(segment_id == 1, rolled, current)
        result = window_layer(current, gain_row, qkv_local, allowed, project)
        passed = shifted(result, "segment", 1)
        return (passed, result)

    start_slab = jnp.zeros(inputs.shape[1:], jnp.bfloat16)
    _, produced = lax.scan(advance, start_slab, jnp.arange(micro_count + 1, dtype=jnp.int32))
    sections = lax.dynamic_slice_in_dim(produced, segment_id, micro_count, 0)
    return sections[None]


def solution(mesh):
    in_specs = (
        P(None, None, "win", "head"),
        P("segment", None),
        P("segment", None, None, "head"),
        P("segment", "head", None),
        P(None, "win"),
    )
    out_specs = P("segment", None, None, "win", "head")
    return jax.shard_map(body, mesh=mesh, in_specs=in_specs, out_specs=out_specs, check_vma=False)
```

profile of v0, /device:TPU:0, one launch (start us, length us, event | category | flops | bytes accessed | tf_op | source)
XLA Modules:
  0.0 619.6 jit_solution(4641840400463781002)
XLA Ops:
  10.2 598.5 %while.16 = (s32[]{:T(128)}, bf16[30,30,384]{2,1,0:T(8,128)(2,1)S(1)}, bf16[3,30,30,384]{3,2,1,0:T(8,128)(2,1)}, pred[]{:T(512)}, pred[]{:T(512)}, /*index=5*/s3...) while((s32[]{:T(128)}, ...), condition=%wide.region_5.6_spmd.clone.clone, body=%wide.region_0.5_spmd.clone.clone.sunk | while | flops 5522992128 | bytes 120185344 | solution.py:110
  16.8 5.0 collective-permute-done
  24.8 38.2 %all-gather.2.cloned.1.call-done = bf16[30,30,1536]{2,1,0:T(8,128)(2,1)} async-done(((bf16[30,30,384]{2,1,0:T(8,128)(2,1)}), bf16[30,30,1536]{2,1,0:T(8,128)(2,1)}) %all-gather.2.cloned.1.call-update) | async-done | bytes 2764816 | tf_op jit(solution)/shard_map/while/body/eval_jaxpr/all_gather | solution.py:49
  68.7 7.9 %convolution_convert_fusion.4 = bf16[900,3,384]{2,0,1:T(8,128)(2,1)} fusion(bf16[900,1536,1]{1,0,2:T(8,128)(2,1)} %reshape.166, bf16[1536,3,384]{2,0,1:T(8,128)(2,1)} %get-tuple-element.361), kind=kOutput, calls=%fused_computation.17.clone.1 | convolution fusion | flops 3186086400 | bytes 8377344 | tf_op jit(solution)/shard_map/while/body/eval_jaxpr/wtd,dcf->wtcf/dot_general | solution.py:52
  79.5 7.3 %fusion.40 = (f32[3,900]{1,0:T(4,128)S(1)}, f32[3,900,900]{1,2,0:T(8,128)}) fusion(pred[900,900]{0,1:T(8,128)(4,1)S(1)} %copy-done.1, bf16[1,900,3,3,128]{1,4,3,2,0:T(8,128)(2,1)S(1)} %bitcast.85), kind=kOutput, calls=%fused_computation.36.clone.1 | convolution fusion | flops 631800960 | bytes 12229360 | tf_op jit(solution)/shard_map/while/body/eval_jaxpr/sub | solution.py:68
  86.8 6.4 %fusion.41 = bf16[1,900,3,128]{3,1,2,0:T(8,128)(2,1)S(1)} fusion(f32[3,900,900]{1,2,0:T(8,128)} %get-tuple-element.317, f32[3,900]{1,0:T(4,128)S(1)} %get-tuple-element.318, bf16[1,900,3,3,128]{1,4,3,2,0:T(8,128)(2,1)S(1)} %bitcast.86), kind=kOutput, calls=%fused_computation.20.clone.1 | convolution fusion | flops 627285632 | bytes 11214016 | tf_op jit(solution)/shard_map/while/body/eval_jaxpr/whqk,wkhe->wqhe/dot_general | solution.py:70
  98.1 18.7 %copy.42 = bf16[30,30,1536]{1,0,2:T(8,128)(2,1)} copy(bf16[30,30,1536]{2,1,0:T(8,128)(2,1)S(1)} %convolution_convert_fusion.5) | data formatting | bytes 5529600 | tf_op jit(solution)/shard_map/while
  116.8 20.3 %reshape.168 = bf16[1536,900]{1,0:T(8,128)(2,1)} reshape(bf16[1536,30,30]{2,1,0:T(8,128)(2,1)} %bitcast.83) | data formatting | bytes 5529600 | tf_op jit(solution)/shard_map/while
  137.1 38.6 %reduce-scatter.6.cloned.1.call-done = bf16[384,900]{1,0:T(8,128)(2,1)} async-done(((bf16[1536,900]{1,0:T(8,128)(2,1)}), bf16[384,900]{1,0:T(8,128)(2,1)}) %reduce-scatter.6.cloned.1.call-update) | async-done | bytes 691216 | tf_op jit(solution)/shard_map/while
  175.7 8.9 %reshape.169 = bf16[384,30,30]{2,1,0:T(8,128)(2,1)S(1)} reshape(bf16[384,900]{1,0:T(8,128)(2,1)} %reduce-scatter.6.cloned.1.call-done) | data formatting | bytes 1382400 | tf_op jit(solution)/shard_map/while
  191.1 5.1 collective-permute-start.1
  196.2 15.6 %collective-permute-done.1 = bf16[30,30,384]{2,1,0:T(8,128)(2,1)S(1)} collective-permute-done((bf16[30,30,384]{2,1,0:T(8,128)(2,1)S(1)}, bf16[30,30,384]{2,1,0:T(8,128)(2,1)S(1)}, u32[]{:S(2)}, u32[]{:S(2)}) %collective-permute-start.1) | collective-permute-done | bytes 691232 | tf_op jit(solution)/shard_map/while/body/eval_jaxpr/ppermute | solution.py:18
  223.8 37.6 %all-gather.2.cloned.1.call-done = bf16[30,30,1536]{2,1,0:T(8,128)(2,1)} async-done(((bf16[30,30,384]{2,1,0:T(8,128)(2,1)}), bf16[30,30,1536]{2,1,0:T(8,128)(2,1)}) %all-gather.2.cloned.1.call-update) | async-done | bytes 2764816 | tf_op jit(solution)/shard_map/while/body/eval_jaxpr/all_gather | solution.py:49
  267.2 7.9 %convolution_convert_fusion.4 = bf16[900,3,384]{2,0,1:T(8,128)(2,1)} fusion(bf16[900,1536,1]{1,0,2:T(8,128)(2,1)} %reshape.166, bf16[1536,3,384]{2,0,1:T(8,128)(2,1)} %get-tuple-element.361), kind=kOutput, calls=%fused_computation.17.clone.1 | convolution fusion | flops 3186086400 | bytes 8377344 | tf_op jit(solution)/shard_map/while/body/eval_jaxpr/wtd,dcf->wtcf/dot_general | solution.py:52
  278.0 7.4 %fusion.40 = (f32[3,900]{1,0:T(4,128)S(1)}, f32[3,900,900]{1,2,0:T(8,128)}) fusion(pred[900,900]{0,1:T(8,128)(4,1)S(1)} %copy-done.1, bf16[1,900,3,3,128]{1,4,3,2,0:T(8,128)(2,1)S(1)} %bitcast.85), kind=kOutput, calls=%fused_computation.36.clone.1 | convolution fusion | flops 631800960 | bytes 12229360 | tf_op jit(solution)/shard_map/while/body/eval_jaxpr/sub | solution.py:68
  285.3 6.4 %fusion.41 = bf16[1,900,3,128]{3,1,2,0:T(8,128)(2,1)S(1)} fusion(f32[3,900,900]{1,2,0:T(8,128)} %get-tuple-element.317, f32[3,900]{1,0:T(4,128)S(1)} %get-tuple-element.318, bf16[1,900,3,3,128]{1,4,3,2,0:T(8,128)(2,1)S(1)} %bitcast.86), kind=kOutput, calls=%fused_computation.20.clone.1 | convolution fusion | flops 627285632 | bytes 11214016 | tf_op jit(solution)/shard_map/while/body/eval_jaxpr/whqk,wkhe->wqhe/dot_general | solution.py:70
  296.6 18.7 %copy.42 = bf16[30,30,1536]{1,0,2:T(8,128)(2,1)} copy(bf16[30,30,1536]{2,1,0:T(8,128)(2,1)S(1)} %convolution_convert_fusion.5) | data formatting | bytes 5529600 | tf_op jit(solution)/shard_map/while
  315.3 20.3 %reshape.168 = bf16[1536,900]{1,0:T(8,128)(2,1)} reshape(bf16[1536,30,30]{2,1,0:T(8,128)(2,1)} %bitcast.83) | data formatting | bytes 5529600 | tf_op jit(solution)/shard_map/while
  335.6 38.6 %reduce-scatter.6.cloned.1.call-done = bf16[384,900]{1,0:T(8,128)(2,1)} async-done(((bf16[1536,900]{1,0:T(8,128)(2,1)}), bf16[384,900]{1,0:T(8,128)(2,1)}) %reduce-scatter.6.cloned.1.call-update) | async-done | bytes 691216 | tf_op jit(solution)/shard_map/while
  374.2 8.9 %reshape.169 = bf16[384,30,30]{2,1,0:T(8,128)(2,1)S(1)} reshape(bf16[384,900]{1,0:T(8,128)(2,1)} %reduce-scatter.6.cloned.1.call-done) | data formatting | bytes 1382400 | tf_op jit(solution)/shard_map/while
  389.5 5.1 collective-permute-start.1
  394.6 15.6 %collective-permute-done.1 = bf16[30,30,384]{2,1,0:T(8,128)(2,1)S(1)} collective-permute-done((bf16[30,30,384]{2,1,0:T(8,128)(2,1)S(1)}, bf16[30,30,384]{2,1,0:T(8,128)(2,1)S(1)}, u32[]{:S(2)}, u32[]{:S(2)}) %collective-permute-start.1) | collective-permute-done | bytes 691232 | tf_op jit(solution)/shard_map/while/body/eval_jaxpr/ppermute | solution.py:18
  422.2 37.6 %all-gather.2.cloned.1.call-done = bf16[30,30,1536]{2,1,0:T(8,128)(2,1)} async-done(((bf16[30,30,384]{2,1,0:T(8,128)(2,1)}), bf16[30,30,1536]{2,1,0:T(8,128)(2,1)}) %all-gather.2.cloned.1.call-update) | async-done | bytes 2764816 | tf_op jit(solution)/shard_map/while/body/eval_jaxpr/all_gather | solution.py:49
  465.6 7.9 %convolution_convert_fusion.4 = bf16[900,3,384]{2,0,1:T(8,128)(2,1)} fusion(bf16[900,1536,1]{1,0,2:T(8,128)(2,1)} %reshape.166, bf16[1536,3,384]{2,0,1:T(8,128)(2,1)} %get-tuple-element.361), kind=kOutput, calls=%fused_computation.17.clone.1 | convolution fusion | flops 3186086400 | bytes 8377344 | tf_op jit(solution)/shard_map/while/body/eval_jaxpr/wtd,dcf->wtcf/dot_general | solution.py:52
  476.4 7.4 %fusion.40 = (f32[3,900]{1,0:T(4,128)S(1)}, f32[3,900,900]{1,2,0:T(8,128)}) fusion(pred[900,900]{0,1:T(8,128)(4,1)S(1)} %copy-done.1, bf16[1,900,3,3,128]{1,4,3,2,0:T(8,128)(2,1)S(1)} %bitcast.85), kind=kOutput, calls=%fused_computation.36.clone.1 | convolution fusion | flops 631800960 | bytes 12229360 | tf_op jit(solution)/shard_map/while/body/eval_jaxpr/sub | solution.py:68
  483.8 6.4 %fusion.41 = bf16[1,900,3,128]{3,1,2,0:T(8,128)(2,1)S(1)} fusion(f32[3,900,900]{1,2,0:T(8,128)} %get-tuple-element.317, f32[3,900]{1,0:T(4,128)S(1)} %get-tuple-element.318, bf16[1,900,3,3,128]{1,4,3,2,0:T(8,128)(2,1)S(1)} %bitcast.86), kind=kOutput, calls=%fused_computation.20.clone.1 | convolution fusion | flops 627285632 | bytes 11214016 | tf_op jit(solution)/shard_map/while/body/eval_jaxpr/whqk,wkhe->wqhe/dot_general | solution.py:70
  495.0 18.7 %copy.42 = bf16[30,30,1536]{1,0,2:T(8,128)(2,1)} copy(bf16[30,30,1536]{2,1,0:T(8,128)(2,1)S(1)} %convolution_convert_fusion.5) | data formatting | bytes 5529600 | tf_op jit(solution)/shard_map/while
  513.7 20.3 %reshape.168 = bf16[1536,900]{1,0:T(8,128)(2,1)} reshape(bf16[1536,30,30]{2,1,0:T(8,128)(2,1)} %bitcast.83) | data formatting | bytes 5529600 | tf_op jit(solution)/shard_map/while
  534.1 38.6 %reduce-scatter.6.cloned.1.call-done = bf16[384,900]{1,0:T(8,128)(2,1)} async-done(((bf16[1536,900]{1,0:T(8,128)(2,1)}), bf16[384,900]{1,0:T(8,128)(2,1)}) %reduce-scatter.6.cloned.1.call-update) | async-done | bytes 691216 | tf_op jit(solution)/shard_map/while
  572.6 8.9 %reshape.169 = bf16[384,30,30]{2,1,0:T(8,128)(2,1)S(1)} reshape(bf16[384,900]{1,0:T(8,128)(2,1)} %reduce-scatter.6.cloned.1.call-done) | data formatting | bytes 1382400 | tf_op jit(solution)/shard_map/while
  588.0 5.1 collective-permute-start.1
  593.0 15.6 %collective-permute-done.1 = bf16[30,30,384]{2,1,0:T(8,128)(2,1)S(1)} collective-permute-done((bf16[30,30,384]{2,1,0:T(8,128)(2,1)S(1)}, bf16[30,30,384]{2,1,0:T(8,128)(2,1)S(1)}, u32[]{:S(2)}, u32[]{:S(2)}) %collective-permute-start.1) | collective-permute-done | bytes 691232 | tf_op jit(solution)/shard_map/while/body/eval_jaxpr/ppermute | solution.py:18
  (86 shorter events, 98.8 us)
Async XLA Ops:
  6.5 3.6 copy-start.2
  10.2 52.8 %all-gather.2.cloned.1.call-start = ((), (), s32[]{:S(2)}) async-start(), calls=%async_computation.1 | async-start | bytes 3686400 | tf_op jit(solution)/shard_map/while/body/eval_jaxpr/all_gather | solution.py:49
  12.8 9.0 %collective-permute-start = (bf16[30,15,384]{2,1,0:T(8,128)(2,1)S(1)}, bf16[30,15,384]{2,1,0:T(8,128)(2,1)S(1)}, u32[]{:S(2)}, u32[]{:S(2)}) collective-permute-start(bf16[30,15,384]{2,1,0:T(8,128)(2,1)S(1)} %get-tuple-element.315), channel_id=1, source_target_pairs={{0,60},{4,0},{8,4},{12,8},{16,12},{20,16},{24,20},{28,24},{32,28},... | collective-permute-start | bytes 1036808 | tf_op jit(solution)/shard_map/while/body/eval_jaxpr/ppermute | solution.py:12
  23.1 152.6 %reduce-scatter.6.cloned.1.call-start = ((), (), s32[]{:S(2)}) async-start(), calls=%async_computation.2 | async-start | bytes 3932160 | tf_op jit(solution)/shard_map/while
  63.0 2.7 copy-start
  76.6 2.9 copy-start.1
  191.1 20.7 %collective-permute-start.1 = (bf16[30,30,384]{2,1,0:T(8,128)(2,1)S(1)}, bf16[30,30,384]{2,1,0:T(8,128)(2,1)S(1)}, u32[]{:S(2)}, u32[]{:S(2)}) collective-permute-start(bf16[30,30,384]{2,1,0:T(8,128)(2,1)S(1)} %get-tuple-element.319), channel_id=1, source_target_pairs={{0,64},{1,65},{2,66},{3,67},{4,68},{5,69},{6,70},{7,71},{8,72},{9,... | collective-permute-start | bytes 2073608 | tf_op jit(solution)/shard_map/while/body/eval_jaxpr/ppermute | solution.py:18
  211.8 49.6 %all-gather.2.cloned.1.call-start = ((), (), s32[]{:S(2)}) async-start(), calls=%async_computation.1 | async-start | bytes 3686400 | tf_op jit(solution)/shard_map/while/body/eval_jaxpr/all_gather | solution.py:49
  214.4 6.5 %collective-permute-start = (bf16[30,15,384]{2,1,0:T(8,128)(2,1)S(1)}, bf16[30,15,384]{2,1,0:T(8,128)(2,1)S(1)}, u32[]{:S(2)}, u32[]{:S(2)}) collective-permute-start(bf16[30,15,384]{2,1,0:T(8,128)(2,1)S(1)} %get-tuple-element.315), channel_id=1, source_target_pairs={{0,60},{4,0},{8,4},{12,8},{16,12},{20,16},{24,20},{28,24},{32,28},... | collective-permute-start | bytes 1036808 | tf_op jit(solution)/shard_map/while/body/eval_jaxpr/ppermute | solution.py:12
  222.1 152.1 %reduce-scatter.6.cloned.1.call-start = ((), (), s32[]{:S(2)}) async-start(), calls=%async_computation.2 | async-start | bytes 3932160 | tf_op jit(solution)/shard_map/while
  261.4 2.7 copy-start
  275.1 2.9 copy-start.1
  389.5 20.7 %collective-permute-start.1 = (bf16[30,30,384]{2,1,0:T(8,128)(2,1)S(1)}, bf16[30,30,384]{2,1,0:T(8,128)(2,1)S(1)}, u32[]{:S(2)}, u32[]{:S(2)}) collective-permute-start(bf16[30,30,384]{2,1,0:T(8,128)(2,1)S(1)} %get-tuple-element.319), channel_id=1, source_target_pairs={{0,64},{1,65},{2,66},{3,67},{4,68},{5,69},{6,70},{7,71},{8,72},{9,... | collective-permute-start | bytes 2073608 | tf_op jit(solution)/shard_map/while/body/eval_jaxpr/ppermute | solution.py:18
  410.2 49.6 %all-gather.2.cloned.1.call-start = ((), (), s32[]{:S(2)}) async-start(), calls=%async_computation.1 | async-start | bytes 3686400 | tf_op jit(solution)/shard_map/while/body/eval_jaxpr/all_gather | solution.py:49
  412.8 6.5 %collective-permute-start = (bf16[30,15,384]{2,1,0:T(8,128)(2,1)S(1)}, bf16[30,15,384]{2,1,0:T(8,128)(2,1)S(1)}, u32[]{:S(2)}, u32[]{:S(2)}) collective-permute-start(bf16[30,15,384]{2,1,0:T(8,128)(2,1)S(1)} %get-tuple-element.315), channel_id=1, source_target_pairs={{0,60},{4,0},{8,4},{12,8},{16,12},{20,16},{24,20},{28,24},{32,28},... | collective-permute-start | bytes 1036808 | tf_op jit(solution)/shard_map/while/body/eval_jaxpr/ppermute | solution.py:12
  420.6 152.1 %reduce-scatter.6.cloned.1.call-start = ((), (), s32[]{:S(2)}) async-start(), calls=%async_computation.2 | async-start | bytes 3932160 | tf_op jit(solution)/shard_map/while
  459.9 2.7 copy-start
  473.5 2.9 copy-start.1
  588.0 20.7 %collective-permute-start.1 = (bf16[30,30,384]{2,1,0:T(8,128)(2,1)S(1)}, bf16[30,30,384]{2,1,0:T(8,128)(2,1)S(1)}, u32[]{:S(2)}, u32[]{:S(2)}) collective-permute-start(bf16[30,30,384]{2,1,0:T(8,128)(2,1)S(1)} %get-tuple-element.319), channel_id=1, source_target_pairs={{0,64},{1,65},{2,66},{3,67},{4,68},{5,69},{6,70},{7,71},{8,72},{9,... | collective-permute-start | bytes 2073608 | tf_op jit(solution)/shard_map/while/body/eval_jaxpr/ppermute | solution.py:18
Sparse Core Ops, SparseCore 0:
  23.2 39.6 all-gather.1
  137.3 38.4 reduce-scatter.5
  222.2 39.1 all-gather.1
  335.7 38.4 reduce-scatter.5
  420.7 39.1 all-gather.1
  534.2 38.4 reduce-scatter.5
where the time goes:
time: 621 us; the launch traced here: 620 us
  waiting for transfers between devices  291 us (47%)
  local copies, waits for them, and re-layouts  186 us (30%)
  matrix products  74.5 us (12%)
  other arithmetic  29.7 us (5%)
  starting transfers between devices  22.3 us (4%)
  between operations  13.4 us (2%)
    while x24, local copies, waits for them, and re-layouts  156 us
    while x9, waiting for transfers between devices  116 us
    all_gather x3, waiting for transfers between devices, window_layer(): gathered = lax.all_gather(current, 'head', axis=2, tiled=True)  113 us
    ppermute x3, waiting for transfers between devices, shifted(): lax.ppermute(value, axis, [(source, source + steps) for source in range(f...  46.9 us
    dot_general x3, matrix products, window_layer(): jnp.einsum('wtd,dcf->wtcf', win_normed, qkv_local, preferred_element_type...  23.8 us
    sub x3, matrix products, window_layer(): expo = jnp.exp(scores - top_score)  22.1 us
    dot_general x3, matrix products, window_layer(): jnp.einsum('whqk,wkhe->wqhe', attn_prob, values_all, preferred_element_ty...  19.1 us
    ppermute x3, starting transfers between devices, shifted(): lax.ppermute(value, axis, [(source, source + steps) for source in range(f...  15.2 us
  transfers between devices with their start and end apart: 12, of which 12 were waited for; matrix products, arithmetic and copies ran while one was open for 1% of the time, Pallas kernels for 0%

commit v1 on v0

--- a/solution.py
+++ b/solution.py
@@ -46,7 +46,9 @@
 
 
 def window_layer(current, gain_row, qkv_local, allowed, project):
-    gathered = lax.all_gather(current, "head", axis=2, tiled=True)
+    gathered = jnp.concatenate(
+        lax.all_to_all(jnp.stack([current] * lax.axis_size("head")), "head", 0, 0), axis=2
+    )
     normed = rms_normed(gathered, gain_row)
     win_normed = to_windows(normed)
     projected_qkv = jnp.einsum(

time: 621 us -> 640 us (1.031)
  local copies, waits for them, and re-layouts: 186 us -> 213 us
  waiting for transfers between devices: 291 us -> 277 us
  starting transfers between devices: 22.3 us -> 33.9 us
  other arithmetic: 29.7 us -> 21.3 us
    all_gather x3 -> x0, waiting for transfers between devices: 113 us -> none  [window_layer(): gathered = lax.all_gather(current, 'head', axis=2, tiled=True)]
    all_to_all x0 -> x3, waiting for transfers between devices: none -> 100 us  [window_layer(): lax.all_to_all(jnp.stack([current] * lax.axis_size('head')), 'head', 0, 0)]
    convert_element_type x0 -> x3, local copies, waits for them, and re-layouts: none -> 13.8 us  [rms_normed(): values_f = slab.astype(jnp.float32)]
    while x24 -> x30, local copies, waits for them, and re-layouts: 156 us -> 170 us
    all_to_all x0 -> x3, starting transfers between devices: none -> 11.7 us  [window_layer(): lax.all_to_all(jnp.stack([current] * lax.axis_size('head')), 'head', 0, 0)]
    while x9 -> x6, waiting for transfers between devices: 116 us -> 115 us
where the time goes in v1:
time: 640 us; the launch traced here: 638 us
  waiting for transfers between devices  277 us (43%)
  local copies, waits for them, and re-layouts  213 us (33%)
  matrix products  77.7 us (12%)
  starting transfers between devices  33.9 us (5%)
  other arithmetic  21.3 us (3%)
  between operations  13.1 us (2%)
    while x30, local copies, waits for them, and re-layouts  170 us
    while x6, waiting for transfers between devices  115 us
    all_to_all x3, waiting for transfers between devices, window_layer(): lax.all_to_all(jnp.stack([current] * lax.axis_size('head')), 'head', 0, 0)  100 us
    ppermute x3, waiting for transfers between devices, shifted(): lax.ppermute(value, axis, [(source, source + steps) for source in range(f...  46.9 us
    dot_general x3, matrix products, window_layer(): jnp.einsum('wtd,dcf->wtcf', win_normed, qkv_local, preferred_element_type...  26.8 us
    sub x3, matrix products, window_layer(): expo = jnp.exp(scores - top_score)  22.3 us
    dot_general x3, matrix products, window_layer(): jnp.einsum('whqk,wkhe->wqhe', attn_prob, values_all, preferred_element_ty...  19.1 us
    ppermute x3, starting transfers between devices, shifted(): lax.ppermute(value, axis, [(source, source + steps) for source in range(f...  15.3 us
  transfers between devices with their start and end apart: 12, of which 12 were waited for; matrix products, arithmetic and copies ran while one was open for 1% of the time, Pallas kernels for 0%

profile of v1, /device:TPU:0, one launch (start us, length us, event | category | flops | bytes accessed | tf_op | source)
XLA Modules:
  0.0 638.2 jit_solution(2694059572702554380)
XLA Ops:
  10.2 617.5 %while.16 = (s32[]{:T(128)}, bf16[30,30,384]{2,1,0:T(8,128)(2,1)S(1)}, bf16[3,30,30,384]{3,2,1,0:T(8,128)(2,1)}, pred[]{:T(512)}, pred[]{:T(512)}, /*index=5*/s3...) while((s32[]{:T(128)}, ...), condition=%wide.region_5.6_spmd.clone.clone, body=%wide.region_0.5_spmd.clone.clone.sunk | while | flops 5522992128 | bytes 146670096 | solution.py:112
  16.8 5.0 collective-permute-done
  30.8 32.4 %all-to-all-done = bf16[4,30,30,384]{3,2,1,0:T(8,128)(2,1)S(1)} async-done(((bf16[4,30,30,384]{3,2,1,0:T(8,128)(2,1)}), bf16[4,30,30,384]{3,2,1,0:T(8,128)(2,1)S(1)}, u32[]{:S(2)}, u32[]{:S(2)}) %all-to-all-start) | async-done | bytes 2764832 | tf_op jit(solution)/shard_map/while/body/eval_jaxpr/all_to_all | solution.py:50
  73.3 8.9 %fusion.44 = bf16[900,3,384]{2,0,1:T(8,128)(2,1)} fusion(bf16[1536,3,384]{2,0,1:T(8,128)(2,1)} %get-tuple-element.374, f32[900,1536]{1,0:T(8,128)} %bitcast.105, f32[1536]{0:T(1024)S(1)} %reduce.12, f32[900]{0:T(1024)S(1)} %rsqrt.21), kind=kOutput, calls=%fused_computation.20.clone.1 | convolution fusion | flops 3190233600 | bytes 11151888 | tf_op jit(solution)/shard_map/while/body/eval_jaxpr/wtd,dcf->wtcf/dot_general | solution.py:54
  85.1 7.4 %fusion.45 = (f32[3,900]{1,0:T(4,128)S(1)}, f32[3,900,900]{1,2,0:T(8,128)}) fusion(pred[900,900]{0,1:T(8,128)(4,1)S(1)} %copy-done.1, bf16[1,900,3,3,128]{1,4,3,2,0:T(8,128)(2,1)S(1)} %bitcast.106), kind=kOutput, calls=%fused_computation.39.clone.1 | convolution fusion | flops 631800960 | bytes 12229360 | tf_op jit(solution)/shard_map/while/body/eval_jaxpr/sub | solution.py:70
  92.5 6.4 fusion.46
  103.8 18.7 %copy.56 = bf16[30,30,1536]{1,0,2:T(8,128)(2,1)} copy(bf16[30,30,1536]{2,1,0:T(8,128)(2,1)S(1)} %convolution_convert_fusion.2) | data formatting | bytes 5529600 | tf_op jit(solution)/shard_map/while
  122.5 20.3 %reshape.183 = bf16[1536,900]{1,0:T(8,128)(2,1)} reshape(bf16[1536,30,30]{2,1,0:T(8,128)(2,1)} %bitcast.101) | data formatting | bytes 5529600 | tf_op jit(solution)/shard_map/while
  142.8 38.5 %reduce-scatter.6.cloned.1.call-done = bf16[384,900]{1,0:T(8,128)(2,1)} async-done(((bf16[1536,900]{1,0:T(8,128)(2,1)}), bf16[384,900]{1,0:T(8,128)(2,1)}) %reduce-scatter.6.cloned.1.call-update) | async-done | bytes 691216 | tf_op jit(solution)/shard_map/while
  181.3 8.9 %reshape.184 = bf16[384,30,30]{2,1,0:T(8,128)(2,1)S(1)} reshape(bf16[384,900]{1,0:T(8,128)(2,1)} %reduce-scatter.6.cloned.1.call-done) | data formatting | bytes 1382400 | tf_op jit(solution)/shard_map/while
  196.7 5.1 collective-permute-start.1
  201.8 15.6 %collective-permute-done.1 = bf16[30,30,384]{2,1,0:T(8,128)(2,1)S(1)} collective-permute-done((bf16[30,30,384]{2,1,0:T(8,128)(2,1)S(1)}, bf16[30,30,384]{2,1,0:T(8,128)(2,1)S(1)}, u32[]{:S(2)}, u32[]{:S(2)}) %collective-permute-start.1) | collective-permute-done | bytes 691232 | tf_op jit(solution)/shard_map/while/body/eval_jaxpr/ppermute | solution.py:18
  234.9 33.8 %all-to-all-done = bf16[4,30,30,384]{3,2,1,0:T(8,128)(2,1)S(1)} async-done(((bf16[4,30,30,384]{3,2,1,0:T(8,128)(2,1)}), bf16[4,30,30,384]{3,2,1,0:T(8,128)(2,1)S(1)}, u32[]{:S(2)}, u32[]{:S(2)}) %all-to-all-start) | async-done | bytes 2764832 | tf_op jit(solution)/shard_map/while/body/eval_jaxpr/all_to_all | solution.py:50
  278.8 8.9 %fusion.44 = bf16[900,3,384]{2,0,1:T(8,128)(2,1)} fusion(bf16[1536,3,384]{2,0,1:T(8,128)(2,1)} %get-tuple-element.374, f32[900,1536]{1,0:T(8,128)} %bitcast.105, f32[1536]{0:T(1024)S(1)} %reduce.12, f32[900]{0:T(1024)S(1)} %rsqrt.21), kind=kOutput, calls=%fused_computation.20.clone.1 | convolution fusion | flops 3190233600 | bytes 11151888 | tf_op jit(solution)/shard_map/while/body/eval_jaxpr/wtd,dcf->wtcf/dot_general | solution.py:54
  290.6 7.4 %fusion.45 = (f32[3,900]{1,0:T(4,128)S(1)}, f32[3,900,900]{1,2,0:T(8,128)}) fusion(pred[900,900]{0,1:T(8,128)(4,1)S(1)} %copy-done.1, bf16[1,900,3,3,128]{1,4,3,2,0:T(8,128)(2,1)S(1)} %bitcast.106), kind=kOutput, calls=%fused_computation.39.clone.1 | convolution fusion | flops 631800960 | bytes 12229360 | tf_op jit(solution)/shard_map/while/body/eval_jaxpr/sub | solution.py:70
  298.0 6.4 fusion.46
  309.3 18.7 %copy.56 = bf16[30,30,1536]{1,0,2:T(8,128)(2,1)} copy(bf16[30,30,1536]{2,1,0:T(8,128)(2,1)S(1)} %convolution_convert_fusion.2) | data formatting | bytes 5529600 | tf_op jit(solution)/shard_map/while
  328.0 20.3 %reshape.183 = bf16[1536,900]{1,0:T(8,128)(2,1)} reshape(bf16[1536,30,30]{2,1,0:T(8,128)(2,1)} %bitcast.101) | data formatting | bytes 5529600 | tf_op jit(solution)/shard_map/while
  348.3 38.2 %reduce-scatter.6.cloned.1.call-done = bf16[384,900]{1,0:T(8,128)(2,1)} async-done(((bf16[1536,900]{1,0:T(8,128)(2,1)}), bf16[384,900]{1,0:T(8,128)(2,1)}) %reduce-scatter.6.cloned.1.call-update) | async-done | bytes 691216 | tf_op jit(solution)/shard_map/while
  386.5 8.9 %reshape.184 = bf16[384,30,30]{2,1,0:T(8,128)(2,1)S(1)} reshape(bf16[384,900]{1,0:T(8,128)(2,1)} %reduce-scatter.6.cloned.1.call-done) | data formatting | bytes 1382400 | tf_op jit(solution)/shard_map/while
  401.8 5.1 collective-permute-start.1
  406.9 15.6 %collective-permute-done.1 = bf16[30,30,384]{2,1,0:T(8,128)(2,1)S(1)} collective-permute-done((bf16[30,30,384]{2,1,0:T(8,128)(2,1)S(1)}, bf16[30,30,384]{2,1,0:T(8,128)(2,1)S(1)}, u32[]{:S(2)}, u32[]{:S(2)}) %collective-permute-start.1) | collective-permute-done | bytes 691232 | tf_op jit(solution)/shard_map/while/body/eval_jaxpr/ppermute | solution.py:18
  440.1 33.8 %all-to-all-done = bf16[4,30,30,384]{3,2,1,0:T(8,128)(2,1)S(1)} async-done(((bf16[4,30,30,384]{3,2,1,0:T(8,128)(2,1)}), bf16[4,30,30,384]{3,2,1,0:T(8,128)(2,1)S(1)}, u32[]{:S(2)}, u32[]{:S(2)}) %all-to-all-start) | async-done | bytes 2764832 | tf_op jit(solution)/shard_map/while/body/eval_jaxpr/all_to_all | solution.py:50
  483.9 8.9 %fusion.44 = bf16[900,3,384]{2,0,1:T(8,128)(2,1)} fusion(bf16[1536,3,384]{2,0,1:T(8,128)(2,1)} %get-tuple-element.374, f32[900,1536]{1,0:T(8,128)} %bitcast.105, f32[1536]{0:T(1024)S(1)} %reduce.12, f32[900]{0:T(1024)S(1)} %rsqrt.21), kind=kOutput, calls=%fused_computation.20.clone.1 | convolution fusion | flops 3190233600 | bytes 11151888 | tf_op jit(solution)/shard_map/while/body/eval_jaxpr/wtd,dcf->wtcf/dot_general | solution.py:54
  495.7 7.4 %fusion.45 = (f32[3,900]{1,0:T(4,128)S(1)}, f32[3,900,900]{1,2,0:T(8,128)}) fusion(pred[900,900]{0,1:T(8,128)(4,1)S(1)} %copy-done.1, bf16[1,900,3,3,128]{1,4,3,2,0:T(8,128)(2,1)S(1)} %bitcast.106), kind=kOutput, calls=%fused_computation.39.clone.1 | convolution fusion | flops 631800960 | bytes 12229360 | tf_op jit(solution)/shard_map/while/body/eval_jaxpr/sub | solution.py:70
  503.2 6.4 fusion.46
  514.5 18.7 %copy.56 = bf16[30,30,1536]{1,0,2:T(8,128)(2,1)} copy(bf16[30,30,1536]{2,1,0:T(8,128)(2,1)S(1)} %convolution_convert_fusion.2) | data formatting | bytes 5529600 | tf_op jit(solution)/shard_map/while
  533.1 20.3 %reshape.183 = bf16[1536,900]{1,0:T(8,128)(2,1)} reshape(bf16[1536,30,30]{2,1,0:T(8,128)(2,1)} %bitcast.101) | data formatting | bytes 5529600 | tf_op jit(solution)/shard_map/while
  553.5 38.2 %reduce-scatter.6.cloned.1.call-done = bf16[384,900]{1,0:T(8,128)(2,1)} async-done(((bf16[1536,900]{1,0:T(8,128)(2,1)}), bf16[384,900]{1,0:T(8,128)(2,1)}) %reduce-scatter.6.cloned.1.call-update) | async-done | bytes 691216 | tf_op jit(solution)/shard_map/while
  591.6 8.9 %reshape.184 = bf16[384,30,30]{2,1,0:T(8,128)(2,1)S(1)} reshape(bf16[384,900]{1,0:T(8,128)(2,1)} %reduce-scatter.6.cloned.1.call-done) | data formatting | bytes 1382400 | tf_op jit(solution)/shard_map/while
  607.0 5.1 collective-permute-start.1
  612.1 15.6 %collective-permute-done.1 = bf16[30,30,384]{2,1,0:T(8,128)(2,1)S(1)} collective-permute-done((bf16[30,30,384]{2,1,0:T(8,128)(2,1)S(1)}, bf16[30,30,384]{2,1,0:T(8,128)(2,1)S(1)}, u32[]{:S(2)}, u32[]{:S(2)}) %collective-permute-start.1) | collective-permute-done | bytes 691232 | tf_op jit(solution)/shard_map/while/body/eval_jaxpr/ppermute | solution.py:18
  (95 shorter events, 128.9 us)
Async XLA Ops:
  6.5 3.6 copy-start.2
  12.8 9.0 %collective-permute-start = (bf16[30,15,384]{2,1,0:T(8,128)(2,1)S(1)}, bf16[30,15,384]{2,1,0:T(8,128)(2,1)S(1)}, u32[]{:S(2)}, u32[]{:S(2)}) collective-permute-start(bf16[30,15,384]{2,1,0:T(8,128)(2,1)S(1)} %get-tuple-element.326), channel_id=1, source_target_pairs={{0,60},{4,0},{8,4},{12,8},{16,12},{20,16},{24,20},{28,24},{32,28},... | collective-permute-start | bytes 1036808 | tf_op jit(solution)/shard_map/while/body/eval_jaxpr/ppermute | solution.py:12
  22.1 0.9 copy-start
  24.9 38.3 %all-to-all-start = ((bf16[4,30,30,384]{3,2,1,0:T(8,128)(2,1)}), bf16[4,30,30,384]{3,2,1,0:T(8,128)(2,1)S(1)}, u32[]{:S(2)}, u32[]{:S(2)}) async-start(bf16[4,30,30,384]{3,2,1,0:T(8,128)(2,1)} %stack.10), calls=%async_computation | async-start | bytes 5898240 | tf_op jit(solution)/shard_map/while/body/eval_jaxpr/all_to_all | solution.py:50
  29.2 152.1 %reduce-scatter.6.cloned.1.call-start = ((), (), s32[]{:S(2)}) async-start(), calls=%async_computation.2 | async-start | bytes 3932160 | tf_op jit(solution)/shard_map/while
  82.2 2.9 copy-start.1
  196.7 20.7 %collective-permute-start.1 = (bf16[30,30,384]{2,1,0:T(8,128)(2,1)S(1)}, bf16[30,30,384]{2,1,0:T(8,128)(2,1)S(1)}, u32[]{:S(2)}, u32[]{:S(2)}) collective-permute-start(bf16[30,30,384]{2,1,0:T(8,128)(2,1)S(1)} %get-tuple-element.330), channel_id=1, source_target_pairs={{0,64},{1,65},{2,66},{3,67},{4,68},{5,69},{6,70},{7,71},{8,72},{9,... | collective-permute-start | bytes 2073608 | tf_op jit(solution)/shard_map/while/body/eval_jaxpr/ppermute | solution.py:18
  220.0 6.5 %collective-permute-start = (bf16[30,15,384]{2,1,0:T(8,128)(2,1)S(1)}, bf16[30,15,384]{2,1,0:T(8,128)(2,1)S(1)}, u32[]{:S(2)}, u32[]{:S(2)}) collective-permute-start(bf16[30,15,384]{2,1,0:T(8,128)(2,1)S(1)} %get-tuple-element.326), channel_id=1, source_target_pairs={{0,60},{4,0},{8,4},{12,8},{16,12},{20,16},{24,20},{28,24},{32,28},... | collective-permute-start | bytes 1036808 | tf_op jit(solution)/shard_map/while/body/eval_jaxpr/ppermute | solution.py:12
  226.8 0.9 copy-start
  229.6 39.1 %all-to-all-start = ((bf16[4,30,30,384]{3,2,1,0:T(8,128)(2,1)}), bf16[4,30,30,384]{3,2,1,0:T(8,128)(2,1)S(1)}, u32[]{:S(2)}, u32[]{:S(2)}) async-start(bf16[4,30,30,384]{3,2,1,0:T(8,128)(2,1)} %stack.10), calls=%async_computation | async-start | bytes 5898240 | tf_op jit(solution)/shard_map/while/body/eval_jaxpr/all_to_all | solution.py:50
  233.3 153.2 %reduce-scatter.6.cloned.1.call-start = ((), (), s32[]{:S(2)}) async-start(), calls=%async_computation.2 | async-start | bytes 3932160 | tf_op jit(solution)/shard_map/while
  287.7 2.9 copy-start.1
  401.8 20.7 %collective-permute-start.1 = (bf16[30,30,384]{2,1,0:T(8,128)(2,1)S(1)}, bf16[30,30,384]{2,1,0:T(8,128)(2,1)S(1)}, u32[]{:S(2)}, u32[]{:S(2)}) collective-permute-start(bf16[30,30,384]{2,1,0:T(8,128)(2,1)S(1)} %get-tuple-element.330), channel_id=1, source_target_pairs={{0,64},{1,65},{2,66},{3,67},{4,68},{5,69},{6,70},{7,71},{8,72},{9,... | collective-permute-start | bytes 2073608 | tf_op jit(solution)/shard_map/while/body/eval_jaxpr/ppermute | solution.py:18
  425.1 6.5 %collective-permute-start = (bf16[30,15,384]{2,1,0:T(8,128)(2,1)S(1)}, bf16[30,15,384]{2,1,0:T(8,128)(2,1)S(1)}, u32[]{:S(2)}, u32[]{:S(2)}) collective-permute-start(bf16[30,15,384]{2,1,0:T(8,128)(2,1)S(1)} %get-tuple-element.326), channel_id=1, source_target_pairs={{0,60},{4,0},{8,4},{12,8},{16,12},{20,16},{24,20},{28,24},{32,28},... | collective-permute-start | bytes 1036808 | tf_op jit(solution)/shard_map/while/body/eval_jaxpr/ppermute | solution.py:12
  431.9 0.9 copy-start
  434.7 39.1 %all-to-all-start = ((bf16[4,30,30,384]{3,2,1,0:T(8,128)(2,1)}), bf16[4,30,30,384]{3,2,1,0:T(8,128)(2,1)S(1)}, u32[]{:S(2)}, u32[]{:S(2)}) async-start(bf16[4,30,30,384]{3,2,1,0:T(8,128)(2,1)} %stack.10), calls=%async_computation | async-start | bytes 5898240 | tf_op jit(solution)/shard_map/while/body/eval_jaxpr/all_to_all | solution.py:50
  438.4 153.2 %reduce-scatter.6.cloned.1.call-start = ((), (), s32[]{:S(2)}) async-start(), calls=%async_computation.2 | async-start | bytes 3932160 | tf_op jit(solution)/shard_map/while
  492.9 2.9 copy-start.1
  607.0 20.7 %collective-permute-start.1 = (bf16[30,30,384]{2,1,0:T(8,128)(2,1)S(1)}, bf16[30,30,384]{2,1,0:T(8,128)(2,1)S(1)}, u32[]{:S(2)}, u32[]{:S(2)}) collective-permute-start(bf16[30,30,384]{2,1,0:T(8,128)(2,1)S(1)} %get-tuple-element.330), channel_id=1, source_target_pairs={{0,64},{1,65},{2,66},{3,67},{4,68},{5,69},{6,70},{7,71},{8,72},{9,... | collective-permute-start | bytes 2073608 | tf_op jit(solution)/shard_map/while/body/eval_jaxpr/ppermute | solution.py:18
Sparse Core Ops, SparseCore 0:
  142.9 38.2 reduce-scatter.5
  348.4 38.0 reduce-scatter.5
  553.6 38.0 reduce-scatter.5
